TPU v7x, 32 devices: a whole 2x2x4 slice. The times are simulated.
32 devices in a mesh: segment: 2 (over x), seq: 4 (over y, core), head: 4 (over z).
Axes of the slice: x: 2, y: 2, z: 4, core: 2. Of those that a mesh axis runs over, the one named last changes fastest.
Arguments:
- stream: bfloat16 [2, 512, 4096], P(None, 'seq', 'head'), may hold values from -6 to 6
- in_gain: float32 [2, 4096], P('segment'), may hold values from 0.25 to 1.75
- w_qkv: bfloat16 [2, 4096, 4, 3, 512], P('segment', None, 'head'), may hold values from -0.09375 to 0.09375
- qk_gain: float32 [2, 4, 2, 512], P('segment', 'head'), may hold values from 0.25 to 1.75
- w_one: bfloat16 [2, 4, 512, 768], P('segment', 'head'), may hold values from -0.25 to 0.25
- w_three: bfloat16 [2, 4, 512, 768], P('segment', 'head'), may hold values from -0.25 to 0.25
- w_two: bfloat16 [2, 4, 768, 512], P('segment', 'head'), may hold values from -0.21875 to 0.21875
- token_rate: float32 [2, 2, 512], P('segment', None, 'seq'), may hold values from 0.05 to 1
- out_gain: float32 [2, 4, 512], P('segment', 'head'), may hold values from 0.25 to 1.75
- w_out: bfloat16 [2, 4, 512, 4096], P('segment', 'head'), may hold values from -0.125 to 0.125
Outputs:
- sections_out: bfloat16 [2, 2, 512, 4096], P('segment', None, 'seq', 'head')
All inputs are finite; a program needn't handle non-finite values.
Results may differ from a plain program's by a relative error of at most 0.038.
Values may be sent and summed in bfloat16 or wider, within the bound.
A program may use at most 128 MiB of HBM per device.

v0:
```python
import jax
import jax.numpy as jnp
from jax import lax
from jax.sharding import PartitionSpec as P

NS_STEPS = 2
ns_first = 3.4445
ns_second = -4.775
ns_third = 2.0315
update_step = 1.0
norm_eps = 1e-06
grad_eps = 1e-07


def shifted(array, axis, by):
    devices = lax.axis_size(axis)
    pairs = [(i, i + by) for i in range(devices) if 0 <= i + by < devices]
    return lax.ppermute(array, axis, pairs)


def rms_scale(values):
    return values * lax.rsqrt(jnp.mean(values * values, axis=-1, keepdims=True) + norm_eps)


def contract_rows(left, right):
    return lax.dot_general(
        left, right, (((0,), (0,)), ((), ())), preferred_element_type=jnp.float32
    )


def renormalize(weights, target_norms):
    return weights * (target_norms / (jnp.sqrt(jnp.sum(weights * weights, axis=0)) + norm_eps))


def orthogonal_updates(shares):
    squares = jnp.stack([jnp.sum(share * share) for share in shares])
    totals = lax.psum(squares, "seq")
    current = [
        (shares[index] / (jnp.sqrt(totals[index]) + grad_eps)).astype(jnp.bfloat16)
        for index in range(3)
    ]
    for sweep_index in range(NS_STEPS):
        partial_grams = jnp.stack(
            [
                lax.dot_general(
                    block, block, (((1,), (1,)), ((), ())), preferred_element_type=jnp.float32
                )
                .astype(jnp.bfloat16)
                .astype(jnp.float32)
                for block in current
            ]
        )
        grams = lax.psum(partial_grams.astype(jnp.bfloat16), "seq")
        following = []
        for index in range(3):
            gram_matrix = grams[index]
            square = jnp.dot(gram_matrix, gram_matrix, preferred_element_type=jnp.float32)
            mixing = (ns_second * gram_matrix.astype(jnp.float32) + ns_third * square).astype(
                jnp.bfloat16
            )
            block = current[index]
            following.append(
                (
                    ns_first * block.astype(jnp.float32)
                    + jnp.dot(mixing, block, preferred_element_type=jnp.float32)
                ).astype(jnp.bfloat16)
            )
        current = following
    return (
        lax.all_gather(current[0], "seq", axis=1, tiled=True),
        lax.all_gather(current[1], "seq", axis=1, tiled=True),
        lax.all_gather(current[2], "seq", axis=1, tiled=True),
    )


def run_section(
    residual, gain_row, qkv_matrix, head_gains, rate_row, out_gain_row, out_weights, fasts, norms
):
    values = residual.astype(jnp.float32)
    head_width = head_gains.shape[-1]
    whole = lax.all_gather(residual, "head", axis=1, tiled=True)
    normed = (rms_scale(whole.astype(jnp.float32)) * gain_row).astype(jnp.bfloat16)
    projected = jnp.dot(normed, qkv_matrix, preferred_element_type=jnp.float32)
    projected = projected.reshape(residual.shape[0], 3, head_width)
    queries = rms_scale(projected[:, 0]) * head_gains[0]
    key_rows = (rms_scale(projected[:, 1]) * head_gains[1]).astype(jnp.bfloat16)
    out_grad = (-rate_row[:, None] * projected[:, 2]).astype(jnp.bfloat16)
    gate_fast, up_fast, down_fast = fasts
    gate_low = gate_fast.astype(jnp.bfloat16)
    up_low = up_fast.astype(jnp.bfloat16)
    down_low = down_fast.astype(jnp.bfloat16)
    pre_gate = jnp.dot(key_rows, gate_low, preferred_element_type=jnp.float32)
    pre_up = jnp.dot(key_rows, up_low, preferred_element_type=jnp.float32)
    sigmoid_gate = jax.nn.sigmoid(pre_gate)
    gated = pre_gate * sigmoid_gate
    hidden = (gated * pre_up).astype(jnp.bfloat16)
    backward = lax.dot_general(
        out_grad, down_low, (((1,), (1,)), ((), ())), preferred_element_type=jnp.float32
    )
    grad_gate = (backward * pre_up * sigmoid_gate * (1.0 + pre_gate * (1.0 - sigmoid_gate))).astype(
        jnp.bfloat16
    )
    grad_up = (backward * gated).astype(jnp.bfloat16)
    all_keys, all_grads = (
        lax.all_gather(key_rows, "seq", axis=0, tiled=True),
        lax.all_gather(out_grad, "seq", axis=0, tiled=True),
    )
    hidden_part, gate_part, up_part = (
        lax.all_to_all(hidden, "seq", split_axis=1, concat_axis=0, tiled=True),
        lax.all_to_all(grad_gate, "seq", split_axis=1, concat_axis=0, tiled=True),
        lax.all_to_all(grad_up, "seq", split_axis=1, concat_axis=0, tiled=True),
    )
    shares = (
        contract_rows(all_keys, gate_part),
        contract_rows(all_keys, up_part),
        contract_rows(all_grads, hidden_part),
    )
    gate_step, up_step, down_step = orthogonal_updates(shares)
    gate_fast = renormalize(gate_fast - update_step * gate_step.astype(jnp.float32), norms[0])
    up_fast = renormalize(up_fast - update_step * up_step.astype(jnp.float32), norms[1])
    down_fast = renormalize(down_fast - update_step * down_step.astype(jnp.float32).T, norms[2])
    gate_out = jnp.dot(queries, gate_fast, precision=lax.Precision.HIGHEST)
    up_out = jnp.dot(queries, up_fast, precision=lax.Precision.HIGHEST)
    output = jnp.dot(jax.nn.silu(gate_out) * up_out, down_fast, precision=lax.Precision.HIGHEST)
    normed_out = (rms_scale(output) * out_gain_row).astype(jnp.bfloat16)
    head_terms = jnp.dot(normed_out, out_weights, preferred_element_type=jnp.float32)
    delta = lax.psum_scatter(
        head_terms.astype(jnp.bfloat16), "head", scatter_dimension=1, tiled=True
    ).astype(jnp.float32)
    return ((values + delta).astype(jnp.bfloat16), (gate_fast, up_fast, down_fast))


def shards(stream, in_gain, w_qkv, qk_gain, w_one, w_three, w_two, token_rate, out_gain, w_out):
    segment_index = lax.axis_index("segment")
    span_count = stream.shape[0]
    moments = span_count + lax.axis_size("segment") - 1
    qkv_matrix = w_qkv[0].reshape(w_qkv.shape[1], -1)
    fasts = (
        w_one[0, 0].astype(jnp.float32),
        w_three[0, 0].astype(jnp.float32),
        w_two[0, 0].astype(jnp.float32),
    )
    norms = tuple((jnp.sqrt(jnp.sum(matrix * matrix, axis=0)) for matrix in fasts))
    received = jnp.zeros_like(stream[0])
    collected = jnp.zeros(stream.shape, jnp.bfloat16)
    for moment in range(moments):
        span_index = moment - segment_index
        active = (span_index >= 0) & (span_index < span_count)
        clipped = jnp.clip(span_index, 0, span_count - 1)
        source = jnp.where(segment_index == 0, stream[min(moment, span_count - 1)], received)
        rate_row = lax.dynamic_index_in_dim(token_rate[0], clipped, 0, keepdims=False)
        result, updated = run_section(
            source,
            in_gain[0],
            qkv_matrix,
            qk_gain[0, 0],
            rate_row,
            out_gain[0, 0],
            w_out[0, 0],
            fasts,
            norms,
        )
        fasts = tuple((jnp.where(active, fresh, former) for fresh, former in zip(updated, fasts)))
        chosen = jnp.arange(span_count) == span_index
        collected = jnp.where(chosen[:, None, None], result[None], collected)
        if moment + 1 < moments:
            received = shifted(result, "segment", 1)
    return collected[None]


def solution(mesh):
    placed = (
        P(None, "seq", "head"),
        P("segment", None),
        P("segment", None, "head", None, None),
        P("segment", "head", None, None),
        P("segment", "head", None, None),
        P("segment", "head", None, None),
        P("segment", "head", None, None),
        P("segment", None, "seq"),
        P("segment", "head", None),
        P("segment", "head", None, None),
    )
    return jax.shard_map(
        shards,
        mesh=mesh,
        in_specs=placed,
        out_specs=P("segment", None, "seq", "head"),
        check_vma=False,
    )
```

profile of v0, /device:TPU:0, one launch (start us, length us, event | category | flops | bytes accessed | tf_op | source)
XLA Modules:
  0.0 861.6 jit_solution(11526859129735552482)
XLA Ops:
  8.3 17.0 %copy.13 = bf16[1,4096,1,3,512]{1,4,3,2,0:T(8,128)(2,1)} copy(bf16[1,4096,1,3,512]{4,1,3,2,0:T(8,128)(2,1)} %param.12) | data formatting | bytes 25165824 | tf_op args[2]
  26.4 13.3 %all-gather.9.cloned.1.call-done = bf16[1,128,4096]{2,1,0:T(8,128)(2,1)} async-done(((bf16[1,128,1024]{2,1,0:T(8,128)(2,1)}), bf16[1,128,4096]{2,1,0:T(8,128)(2,1)}) %all-gather.9.cloned.1.call-update) | async-done | bytes 1048592 | tf_op jit(solution)/shard_map/all_gather | solution.py:81
  41.3 8.9 %fusion.4 = f32[128,3,512]{2,0,1:T(8,128)S(1)} fusion(bf16[1,4096,1,3,512]{1,4,3,2,0:T(8,128)(2,1)} %copy.13, bf16[1,128,4096]{2,1,0:T(8,128)(2,1)S(1)} %copy-done.31, f32[4096]{0:T(1024)S(1)} %bitcast.605, f32[128]{0:T(128)S(1)} %add_rsqrt_fusion.11), kind=kOutput, calls=%fused_computation.4 | convolution fusion | flops 1612709888 | bytes 14434816 | tf_op jit(solution)/shard_map/dot_general | solution.py:83
  58.3 8.9 %all_gather.55 = bf16[512,512]{1,0:T(8,128)(2,1)S(1)} all-gather(bf16[128,512]{1,0:T(8,128)(2,1)S(1)} %get-tuple-element.30), channel_id=1, replica_groups=mesh['segment'=2,'seq'=4,'head'=4] {'seq'}, dimensions={0}, use_global_device_ids=true | all-gather | bytes 655360 | tf_op jit(solution)/shard_map/all_gather | solution.py:105
  68.9 7.3 all_gather.56
  108.2 41.7 %all-reduce.7.cloned.1.call-done = bf16[3,512,512]{2,1,0:T(8,128)(2,1)} async-done(((bf16[3,512,512]{2,1,0:T(8,128)(2,1)}), bf16[3,512,512]{2,1,0:T(8,128)(2,1)}) %all-reduce.7.cloned.1.call-update) | async-done | bytes 1572880 | tf_op jit(solution)/shard_map/psum | solution.py:53
  162.1 39.8 %all-reduce.9.cloned.1.call-done = bf16[3,512,512]{2,1,0:T(8,128)(2,1)} async-done(((bf16[3,512,512]{2,1,0:T(8,128)(2,1)}), bf16[3,512,512]{2,1,0:T(8,128)(2,1)}) %all-reduce.9.cloned.1.call-update) | async-done | bytes 1572880 | tf_op jit(solution)/shard_map/psum | solution.py:53
  204.0 8.3 all_gather.59
  215.4 8.7 %all_gather.57 = bf16[512,768]{0,1:T(8,128)(2,1)S(1)} all-gather(bf16[512,192]{0,1:T(8,128)(2,1)S(1)} %fusion.155), channel_id=1, replica_groups=mesh['segment'=2,'seq'=4,'head'=4] {'seq'}, dimensions={1}, use_global_device_ids=true | all-gather | bytes 983040 | tf_op jit(solution)/shard_map/all_gather | solution.py:70
  226.4 8.8 %all_gather.58 = bf16[512,768]{0,1:T(8,128)(2,1)S(1)} all-gather(bf16[512,192]{0,1:T(8,128)(2,1)S(1)} %fusion.154), channel_id=1, replica_groups=mesh['segment'=2,'seq'=4,'head'=4] {'seq'}, dimensions={1}, use_global_device_ids=true | all-gather | bytes 983040 | tf_op jit(solution)/shard_map/all_gather | solution.py:71
  244.5 27.9 %reduce-scatter.4.cloned.1.call-done = bf16[128,1024]{1,0:T(8,128)(2,1)} async-done(((bf16[128,4096]{1,0:T(8,128)(2,1)}), bf16[128,1024]{1,0:T(8,128)(2,1)}) %reduce-scatter.4.cloned.1.call-update) | async-done | bytes 262160 | tf_op jit(solution)/shard_map/reduce_scatter | solution.py:127
  284.4 28.0 %all-gather.5.cloned.1.call-done = bf16[128,4096]{1,0:T(8,128)(2,1)} async-done(((bf16[128,1024]{1,0:T(8,128)(2,1)}), bf16[128,4096]{1,0:T(8,128)(2,1)}) %all-gather.5.cloned.1.call-update) | async-done | bytes 1048592 | tf_op jit(solution)/shard_map/all_gather | solution.py:81
  314.1 8.9 %fusion.2 = f32[128,3,512]{2,0,1:T(8,128)S(1)} fusion(bf16[1,4096,1,3,512]{1,4,3,2,0:T(8,128)(2,1)} %copy.13, bf16[128,4096]{1,0:T(8,128)(2,1)S(1)} %copy-done.33, f32[128]{0:T(128)S(1)} %add_rsqrt_fusion.7, f32[4096]{0:T(1024)S(1)} %bitcast.606), kind=kOutput, calls=%fused_computation.2 | convolution fusion | flops 1612709888 | bytes 14434816 | tf_op jit(solution)/shard_map/dot_general | solution.py:83
  323.7 8.0 all_gather.61
  342.0 8.1 all_gather.62
  372.7 6.4 psum.66
  386.1 41.7 %all-reduce.11.cloned.1.call-done = bf16[3,512,512]{2,1,0:T(8,128)(2,1)} async-done(((bf16[3,512,512]{2,1,0:T(8,128)(2,1)}), bf16[3,512,512]{2,1,0:T(8,128)(2,1)}) %all-reduce.11.cloned.1.call-update) | async-done | bytes 1572880 | tf_op jit(solution)/shard_map/psum | solution.py:53
  441.9 41.9 %all-reduce.13.cloned.1.call-done = bf16[3,512,512]{2,1,0:T(8,128)(2,1)} async-done(((bf16[3,512,512]{2,1,0:T(8,128)(2,1)}), bf16[3,512,512]{2,1,0:T(8,128)(2,1)}) %all-reduce.13.cloned.1.call-update) | async-done | bytes 1572880 | tf_op jit(solution)/shard_map/psum | solution.py:53
  486.8 8.4 all_gather.65
  500.8 9.0 %all_gather.63 = bf16[512,768]{0,1:T(8,128)(2,1)S(1)} all-gather(bf16[512,192]{0,1:T(8,128)(2,1)} %fusion.149), channel_id=1, replica_groups=mesh['segment'=2,'seq'=4,'head'=4] {'seq'}, dimensions={1}, use_global_device_ids=true | all-gather | bytes 983040 | tf_op jit(solution)/shard_map/all_gather | solution.py:70
  515.2 9.0 %all_gather.64 = bf16[512,768]{0,1:T(8,128)(2,1)S(1)} all-gather(bf16[512,192]{0,1:T(8,128)(2,1)S(1)} %fusion.148), channel_id=1, replica_groups=mesh['segment'=2,'seq'=4,'head'=4] {'seq'}, dimensions={1}, use_global_device_ids=true | all-gather | bytes 983040 | tf_op jit(solution)/shard_map/all_gather | solution.py:71
  534.4 27.9 %reduce-scatter.6.cloned.1.call-done = bf16[128,1024]{1,0:T(8,128)(2,1)} async-done(((bf16[128,4096]{1,0:T(8,128)(2,1)}), bf16[128,1024]{1,0:T(8,128)(2,1)}) %reduce-scatter.6.cloned.1.call-update) | async-done | bytes 262160 | tf_op jit(solution)/shard_map/reduce_scatter | solution.py:127
  574.3 28.0 %all-gather.7.cloned.1.call-done = bf16[128,4096]{1,0:T(8,128)(2,1)} async-done(((bf16[128,1024]{1,0:T(8,128)(2,1)}), bf16[128,4096]{1,0:T(8,128)(2,1)}) %all-gather.7.cloned.1.call-update) | async-done | bytes 1048592 | tf_op jit(solution)/shard_map/all_gather | solution.py:81
  603.9 9.0 %fusion = f32[128,3,512]{2,0,1:T(8,128)S(1)} fusion(bf16[1,4096,1,3,512]{1,4,3,2,0:T(8,128)(2,1)} %copy.13, bf16[128,4096]{1,0:T(8,128)(2,1)S(1)} %copy-done.32, f32[128]{0:T(128)S(1)} %add_rsqrt_fusion.3, f32[4096]{0:T(1024)S(1)} %bitcast.607), kind=kOutput, calls=%fused_computation | convolution fusion | flops 1612709888 | bytes 14434816 | tf_op jit(solution)/shard_map/dot_general | solution.py:83
  613.2 7.9 all_gather.67
  632.8 8.1 all_gather.68
  674.9 41.7 %all-reduce.15.cloned.1.call-done = bf16[3,512,512]{2,1,0:T(8,128)(2,1)} async-done(((bf16[3,512,512]{2,1,0:T(8,128)(2,1)}), bf16[3,512,512]{2,1,0:T(8,128)(2,1)}) %all-reduce.15.cloned.1.call-update) | async-done | bytes 1572880 | tf_op jit(solution)/shard_map/psum | solution.py:53
  730.1 42.4 %all-reduce.17.cloned.1.call-done = bf16[3,512,512]{2,1,0:T(8,128)(2,1)} async-done(((bf16[3,512,512]{2,1,0:T(8,128)(2,1)}), bf16[3,512,512]{2,1,0:T(8,128)(2,1)}) %all-reduce.17.cloned.1.call-update) | async-done | bytes 1572880 | tf_op jit(solution)/shard_map/psum | solution.py:53
  775.5 8.3 all_gather.71
  789.4 8.9 %all_gather.69 = bf16[512,768]{0,1:T(8,128)(2,1)S(1)} all-gather(bf16[512,192]{0,1:T(8,128)(2,1)} %fusion.143), channel_id=1, replica_groups=mesh['segment'=2,'seq'=4,'head'=4] {'seq'}, dimensions={1}, use_global_device_ids=true | all-gather | bytes 983040 | tf_op jit(solution)/shard_map/all_gather | solution.py:70
  803.6 9.0 %all_gather.70 = bf16[512,768]{0,1:T(8,128)(2,1)S(1)} all-gather(bf16[512,192]{0,1:T(8,128)(2,1)S(1)} %fusion.142), channel_id=1, replica_groups=mesh['segment'=2,'seq'=4,'head'=4] {'seq'}, dimensions={1}, use_global_device_ids=true | all-gather | bytes 983040 | tf_op jit(solution)/shard_map/all_gather | solution.py:71
  824.4 27.9 %reduce-scatter.8.cloned.1.call-done = bf16[128,1024]{1,0:T(8,128)(2,1)} async-done(((bf16[128,4096]{1,0:T(8,128)(2,1)}), bf16[128,1024]{1,0:T(8,128)(2,1)}) %reduce-scatter.8.cloned.1.call-update) | async-done | bytes 262160 | tf_op jit(solution)/shard_map/reduce_scatter | solution.py:127
  (391 shorter events, 260.8 us)
Async XLA Ops:
  6.5 33.1 %all-gather.9.cloned.1.call-start = ((), (), s32[]{:S(2)}) async-start(), calls=%async_computation.23 | async-start | bytes 1310720 | tf_op jit(solution)/shard_map/all_gather | solution.py:81
  8.3 33.0 %copy-start.57 = (f32[1,4096]{1,0:T(1,128)S(1)}, f32[1,4096]{1,0:T(1,128)}, u32[]{:S(2)}) copy-start(f32[1,4096]{1,0:T(1,128)} %param.11) | copy-start | bytes 49156
  54.9 21.2 %all-to-all-start = ((bf16[128,4,192]{0,2,1:T(8,128)(2,1)}), bf16[128,4,192]{0,2,1:T(8,128)(2,1)S(1)}, u32[]{:S(2)}, u32[]{:S(2)}) async-start(bf16[128,4,192]{0,2,1:T(8,128)(2,1)} %bitcast.19), calls=%async_computation | async-start | bytes 393216 | tf_op jit(solution)/shard_map/all_to_all | solution.py:110
  76.1 8.6 %all-to-all-start.1 = ((bf16[128,4,192]{0,2,1:T(8,128)(2,1)}), bf16[128,4,192]{0,2,1:T(8,128)(2,1)S(1)}, u32[]{:S(2)}, u32[]{:S(2)}) async-start(bf16[128,4,192]{0,2,1:T(8,128)(2,1)} %bitcast.22), calls=%async_computation.1 | async-start | bytes 393216 | tf_op jit(solution)/shard_map/all_to_all | solution.py:111
  84.8 8.6 %all-to-all-start.2 = ((bf16[128,4,192]{0,2,1:T(8,128)(2,1)}), bf16[128,4,192]{0,2,1:T(8,128)(2,1)S(1)}, u32[]{:S(2)}, u32[]{:S(2)}) async-start(bf16[128,4,192]{0,2,1:T(8,128)(2,1)} %bitcast.26), calls=%async_computation.2 | async-start | bytes 393216 | tf_op jit(solution)/shard_map/all_to_all | solution.py:109
  88.2 61.7 %all-reduce.7.cloned.1.call-start = ((), (), s32[]{:S(2)}) async-start(), calls=%async_computation.12 | async-start | bytes 3145728 | tf_op jit(solution)/shard_map/psum | solution.py:53
  108.2 44.2 %copy-start.55 = (f32[512,192]{0,1:T(8,128)S(1)}, f32[512,192]{0,1:T(8,128)}, u32[]{:S(2)}) copy-start(f32[512,192]{0,1:T(8,128)} %get-tuple-element.47) | copy-start | bytes 1179652
  108.2 93.7 %all-reduce.9.cloned.1.call-start = ((), (), s32[]{:S(2)}) async-start(), calls=%async_computation.13 | async-start | bytes 3145728 | tf_op jit(solution)/shard_map/psum | solution.py:53
  158.8 113.6 %reduce-scatter.4.cloned.1.call-start = ((), (), s32[]{:S(2)}) async-start(), calls=%async_computation.14 | async-start | bytes 1310720 | tf_op jit(solution)/shard_map/reduce_scatter | solution.py:127
  236.0 96.4 %copy-start.75 = (f32[512]{0:T(512)}, f32[512]{0:T(512)S(1)}, u32[]{:S(2)}) copy-start(f32[512]{0:T(512)S(1)} %add_divide_fusion.11) | copy-start | bytes 6148
  237.1 95.8 %copy-start.58 = (f32[768]{0:T(1024)}, f32[768]{0:T(1024)S(1)}, u32[]{:S(2)}) copy-start(f32[768]{0:T(1024)S(1)} %add_divide_fusion.8) | copy-start | bytes 9220
  237.5 94.2 %copy-start.70 = (f32[768]{0:T(1024)}, f32[768]{0:T(1024)S(1)}, u32[]{:S(2)}) copy-start(f32[768]{0:T(1024)S(1)} %add_divide_fusion.7) | copy-start | bytes 9220
  244.5 67.9 %all-gather.5.cloned.1.call-start = ((), (), s32[]{:S(2)}) async-start(), calls=%async_computation.15 | async-start | bytes 1310720 | tf_op jit(solution)/shard_map/all_gather | solution.py:81
  274.2 8.5 collective-permute-start
  335.2 15.0 %all-to-all-start.3 = ((bf16[128,4,192]{0,2,1:T(8,128)(2,1)}), bf16[128,4,192]{0,2,1:T(8,128)(2,1)S(1)}, u32[]{:S(2)}, u32[]{:S(2)}) async-start(bf16[128,4,192]{0,2,1:T(8,128)(2,1)} %bitcast.54), calls=%async_computation.4 | async-start | bytes 393216 | tf_op jit(solution)/shard_map/all_to_all | solution.py:110
  350.1 8.6 %all-to-all-start.4 = ((bf16[128,4,192]{0,2,1:T(8,128)(2,1)}), bf16[128,4,192]{0,2,1:T(8,128)(2,1)S(1)}, u32[]{:S(2)}, u32[]{:S(2)}) async-start(bf16[128,4,192]{0,2,1:T(8,128)(2,1)} %bitcast.57), calls=%async_computation.5 | async-start | bytes 393216 | tf_op jit(solution)/shard_map/all_to_all | solution.py:111
  358.8 8.6 %all-to-all-start.5 = ((bf16[128,4,192]{0,2,1:T(8,128)(2,1)}), bf16[128,4,192]{0,2,1:T(8,128)(2,1)S(1)}, u32[]{:S(2)}, u32[]{:S(2)}) async-start(bf16[128,4,192]{0,2,1:T(8,128)(2,1)} %bitcast.60), calls=%async_computation.6 | async-start | bytes 393216 | tf_op jit(solution)/shard_map/all_to_all | solution.py:109
  362.2 65.6 %all-reduce.11.cloned.1.call-start = ((), (), s32[]{:S(2)}) async-start(), calls=%async_computation.16 | async-start | bytes 3145728 | tf_op jit(solution)/shard_map/psum | solution.py:53
  386.1 97.8 %all-reduce.13.cloned.1.call-start = ((), (), s32[]{:S(2)}) async-start(), calls=%async_computation.17 | async-start | bytes 3145728 | tf_op jit(solution)/shard_map/psum | solution.py:53
  440.8 121.5 %reduce-scatter.6.cloned.1.call-start = ((), (), s32[]{:S(2)}) async-start(), calls=%async_computation.18 | async-start | bytes 1310720 | tf_op jit(solution)/shard_map/reduce_scatter | solution.py:127
  526.8 94.4 %copy-start.81 = (f32[768]{0:T(1024)}, f32[768]{0:T(1024)S(1)}, u32[]{:S(2)}) copy-start(f32[768]{0:T(1024)S(1)} %add_divide_fusion.5) | copy-start | bytes 9220
  534.4 67.9 %all-gather.7.cloned.1.call-start = ((), (), s32[]{:S(2)}) async-start(), calls=%async_computation.19 | async-start | bytes 1310720 | tf_op jit(solution)/shard_map/all_gather | solution.py:81
  564.0 8.5 collective-permute-start.1
  625.9 15.0 %all-to-all-start.6 = ((bf16[128,4,192]{0,2,1:T(8,128)(2,1)}), bf16[128,4,192]{0,2,1:T(8,128)(2,1)S(1)}, u32[]{:S(2)}, u32[]{:S(2)}) async-start(bf16[128,4,192]{0,2,1:T(8,128)(2,1)} %bitcast.84), calls=%async_computation.8 | async-start | bytes 393216 | tf_op jit(solution)/shard_map/all_to_all | solution.py:110
  640.9 8.6 %all-to-all-start.7 = ((bf16[128,4,192]{0,2,1:T(8,128)(2,1)}), bf16[128,4,192]{0,2,1:T(8,128)(2,1)S(1)}, u32[]{:S(2)}, u32[]{:S(2)}) async-start(bf16[128,4,192]{0,2,1:T(8,128)(2,1)} %bitcast.87), calls=%async_computation.9 | async-start | bytes 393216 | tf_op jit(solution)/shard_map/all_to_all | solution.py:111
  649.5 8.6 %all-to-all-start.8 = ((bf16[128,4,192]{0,2,1:T(8,128)(2,1)}), bf16[128,4,192]{0,2,1:T(8,128)(2,1)S(1)}, u32[]{:S(2)}, u32[]{:S(2)}) async-start(bf16[128,4,192]{0,2,1:T(8,128)(2,1)} %bitcast.90), calls=%async_computation.10 | async-start | bytes 393216 | tf_op jit(solution)/shard_map/all_to_all | solution.py:109
  652.9 63.6 %all-reduce.15.cloned.1.call-start = ((), (), s32[]{:S(2)}) async-start(), calls=%async_computation.20 | async-start | bytes 3145728 | tf_op jit(solution)/shard_map/psum | solution.py:53
  674.8 97.7 %all-reduce.17.cloned.1.call-start = ((), (), s32[]{:S(2)}) async-start(), calls=%async_computation.21 | async-start | bytes 3145728 | tf_op jit(solution)/shard_map/psum | solution.py:53
  729.5 122.8 %reduce-scatter.8.cloned.1.call-start = ((), (), s32[]{:S(2)}) async-start(), calls=%async_computation.22 | async-start | bytes 1310720 | tf_op jit(solution)/shard_map/reduce_scatter | solution.py:127
  730.1 53.7 %copy-start.77 = (f32[512]{0:T(512)S(1)}, f32[512]{0:T(512)}, u32[]{:S(2)}) copy-start(f32[512]{0:T(512)} %copy-done.75) | copy-start | bytes 6148
  730.1 53.7 %copy-start.87 = (f32[512]{0:T(512)S(1)}, f32[512]{0:T(512)}, u32[]{:S(2)}) copy-start(f32[512]{0:T(512)} %add_divide_fusion.10) | copy-start | bytes 6148
  822.5 29.7 %copy-start.40 = (bf16[128,1024]{1,0:T(8,128)(2,1)S(1)}, bf16[128,1024]{1,0:T(8,128)(2,1)}, u32[]{:S(2)}) copy-start(bf16[128,1024]{1,0:T(8,128)(2,1)} %bitcast_select_fusion) | copy-start | bytes 786436
  (93 other events, 588.8 us)
Sparse Core Ops, SparseCore 0:
  8.9 30.6 all-gather.8
  108.3 41.5 all-reduce.6
  158.9 42.9 all-reduce.8
  244.6 27.7 reduce-scatter.3
  284.5 27.8 all-gather.4
  386.2 41.5 all-reduce.10
  440.9 42.9 all-reduce.12
  534.5 27.7 reduce-scatter.5
  574.4 27.8 all-gather.6
  674.9 41.5 all-reduce.14
  729.6 42.8 all-reduce.16
  824.5 27.7 reduce-scatter.7
where the time goes:
time: 873 us; the launch traced here: 862 us
  waiting for transfers between devices  431 us (49%)
  blocking collectives  145 us (17%)
  matrix products  131 us (15%)
  other arithmetic  53 us (6%)
  local copies, waits for them, and re-layouts  42.2 us (5%)
  starting transfers between devices  37.5 us (4%)
  between operations  21.7 us (2%)
    psum x6, waiting for transfers between devices, orthogonal_updates(): grams = lax.psum(partial_grams.astype(jnp.bfloat16), 'seq')  249 us
    reduce_scatter x3, waiting for transfers between devices, run_section(): lax.psum_scatter(head_terms.astype(jnp.bfloat16), 'head', scatter_dimensi...  83.7 us
    all_gather x3, waiting for transfers between devices, run_section(): whole = lax.all_gather(residual, 'head', axis=1, tiled=True)  69.2 us
    dot_general x18, matrix products, orthogonal_updates(): jnp.dot(mixing, block, preferred_element_type=jnp.float32)  43.4 us
    unnamed x207, local copies, waits for them, and re-layouts  27 us
    all_gather x3, blocking collectives, orthogonal_updates(): lax.all_gather(current[1], 'seq', axis=1, tiled=True)  26.8 us
    dot_general x3, matrix products, run_section(): projected = jnp.dot(normed, qkv_matrix, preferred_element_type=jnp.float32)  26.8 us
    all_gather x3, blocking collectives, orthogonal_updates(): lax.all_gather(current[0], 'seq', axis=1, tiled=True)  26.6 us
  transfers between devices with their start and end apart: 23, of which 20 were waited for; matrix products, arithmetic and copies ran while one was open for 5% of the time, Pallas kernels for 0%

commit v1 on v0

--- a/solution.py
+++ b/solution.py
@@ -50,7 +50,7 @@
                 for block in current
             ]
         )
-        grams = lax.psum(partial_grams.astype(jnp.bfloat16), "seq")
+        grams = jnp.sum(lax.all_gather(partial_grams.astype(jnp.bfloat16), "seq"), axis=0)
         following = []
         for index in range(3):
             gram_matrix = grams[index]

time: 873 us -> 901 us (1.032)
  waiting for transfers between devices: 431 us -> 450 us
  other arithmetic: 53 us -> 70.7 us
    all_gather x0 -> x6, waiting for transfers between devices: none -> 270 us  [orthogonal_updates(): lax.all_gather(partial_grams.astype(jnp.bfloat16), 'seq')]
    psum x6 -> x0, waiting for transfers between devices: 249 us -> none  [orthogonal_updates(): grams = lax.psum(partial_grams.astype(jnp.bfloat16), 'seq')]
    reduce_sum x0 -> x6, other arithmetic: none -> 29.9 us  [orthogonal_updates(): jnp.sum(lax.all_gather(partial_grams.astype(jnp.bfloat16), 'seq'), axis=0)]
    unnamed x207 -> x187, local copies, waits for them, and re-layouts: 27 us -> 22.8 us
where the time goes in v1:
time: 901 us; the launch traced here: 890 us
  waiting for transfers between devices  450 us (50%)
  blocking collectives  145 us (16%)
  matrix products  126 us (14%)
  other arithmetic  70.7 us (8%)
  starting transfers between devices  38.9 us (4%)
  local copies, waits for them, and re-layouts  37.8 us (4%)
  between operations  21.1 us (2%)
    all_gather x6, waiting for transfers between devices, orthogonal_updates(): lax.all_gather(partial_grams.astype(jnp.bfloat16), 'seq')  270 us
    reduce_scatter x3, waiting for transfers between devices, run_section(): lax.psum_scatter(head_terms.astype(jnp.bfloat16), 'head', scatter_dimensi...  82.2 us
    all_gather x3, waiting for transfers between devices, run_section(): whole = lax.all_gather(residual, 'head', axis=1, tiled=True)  69.2 us
    dot_general x18, matrix products, orthogonal_updates(): jnp.dot(mixing, block, preferred_element_type=jnp.float32)  39.7 us
    reduce_sum x6, other arithmetic, orthogonal_updates(): jnp.sum(lax.all_gather(partial_grams.astype(jnp.bfloat16), 'seq'), axis=0)  29.9 us
    dot_general x3, matrix products, run_section(): projected = jnp.dot(normed, qkv_matrix, preferred_element_type=jnp.float32)  26.8 us
    all_gather x3, blocking collectives, orthogonal_updates(): lax.all_gather(current[2], 'seq', axis=1, tiled=True)  26.7 us
    all_gather x3, blocking collectives, orthogonal_updates(): lax.all_gather(current[1], 'seq', axis=1, tiled=True)  26.5 us
  transfers between devices with their start and end apart: 23, of which 20 were waited for; matrix products, arithmetic and copies ran while one was open for 5% of the time, Pallas kernels for 0%

profile of v1, /device:TPU:0, one launch (start us, length us, event | category | flops | bytes accessed | tf_op | source)
XLA Modules:
  0.0 889.6 jit_solution(12160732989286323918)
XLA Ops:
  8.3 17.0 %copy.34 = bf16[1,4096,1,3,512]{1,4,3,2,0:T(8,128)(2,1)} copy(bf16[1,4096,1,3,512]{4,1,3,2,0:T(8,128)(2,1)} %param.12) | data formatting | bytes 25165824 | tf_op args[2]
  26.4 13.2 %all-gather.27.cloned.1.call-done = bf16[1,128,4096]{2,1,0:T(8,128)(2,1)} async-done(((bf16[1,128,1024]{2,1,0:T(8,128)(2,1)}), bf16[1,128,4096]{2,1,0:T(8,128)(2,1)}) %all-gather.27.cloned.1.call-update) | async-done | bytes 1048592 | tf_op jit(solution)/shard_map/all_gather | solution.py:81
  41.3 8.9 %fusion.4 = f32[128,3,512]{2,0,1:T(8,128)S(1)} fusion(bf16[1,4096,1,3,512]{1,4,3,2,0:T(8,128)(2,1)} %copy.34, bf16[1,128,4096]{2,1,0:T(8,128)(2,1)S(1)} %copy-done.29, f32[4096]{0:T(1024)S(1)} %bitcast.605, f32[128]{0:T(128)S(1)} %add_rsqrt_fusion.11), kind=kOutput, calls=%fused_computation.4 | convolution fusion | flops 1612709888 | bytes 14434816 | tf_op jit(solution)/shard_map/dot_general | solution.py:83
  58.4 8.9 %all_gather.79 = bf16[512,512]{1,0:T(8,128)(2,1)S(1)} all-gather(bf16[128,512]{1,0:T(8,128)(2,1)S(1)} %get-tuple-element.30), channel_id=1, replica_groups=mesh['segment'=2,'seq'=4,'head'=4] {'seq'}, dimensions={0}, use_global_device_ids=true | all-gather | bytes 655360 | tf_op jit(solution)/shard_map/all_gather | solution.py:105
  68.9 7.3 all_gather.80
  106.9 45.2 %all-gather.11.cloned.1.call-done = bf16[4,3,512,512]{3,2,1,0:T(8,128)(2,1)} async-done(((bf16[1,3,512,512]{3,2,1,0:T(8,128)(2,1)}), bf16[4,3,512,512]{3,2,1,0:T(8,128)(2,1)}) %all-gather.11.cloned.1.call-update) | async-done | bytes 6291472 | tf_op jit(solution)/shard_map/all_gather | solution.py:53
  165.0 43.4 %all-gather.13.cloned.1.call-done = bf16[4,3,512,512]{3,2,1,0:T(8,128)(2,1)} async-done(((bf16[1,3,512,512]{3,2,1,0:T(8,128)(2,1)}), bf16[4,3,512,512]{3,2,1,0:T(8,128)(2,1)}) %all-gather.13.cloned.1.call-update) | async-done | bytes 6291472 | tf_op jit(solution)/shard_map/all_gather | solution.py:53
  217.0 8.9 %all_gather.85 = bf16[512,768]{0,1:T(8,128)(2,1)S(1)} all-gather(bf16[512,192]{0,1:T(8,128)(2,1)} %fusion.153), channel_id=1, replica_groups=mesh['segment'=2,'seq'=4,'head'=4] {'seq'}, dimensions={1}, use_global_device_ids=true | all-gather | bytes 983040 | tf_op jit(solution)/shard_map/all_gather | solution.py:72
  226.4 8.8 all_gather.83
  235.2 8.7 all_gather.84
  252.3 27.4 %reduce-scatter.4.cloned.1.call-done = bf16[128,1024]{1,0:T(8,128)(2,1)} async-done(((bf16[128,4096]{1,0:T(8,128)(2,1)}), bf16[128,1024]{1,0:T(8,128)(2,1)}) %reduce-scatter.4.cloned.1.call-update) | async-done | bytes 262160 | tf_op jit(solution)/shard_map/reduce_scatter | solution.py:127
  291.7 28.0 %all-gather.15.cloned.1.call-done = bf16[128,4096]{1,0:T(8,128)(2,1)} async-done(((bf16[128,1024]{1,0:T(8,128)(2,1)}), bf16[128,4096]{1,0:T(8,128)(2,1)}) %all-gather.15.cloned.1.call-update) | async-done | bytes 1048592 | tf_op jit(solution)/shard_map/all_gather | solution.py:81
  321.3 8.9 %fusion.2 = f32[128,3,512]{2,0,1:T(8,128)S(1)} fusion(bf16[1,4096,1,3,512]{1,4,3,2,0:T(8,128)(2,1)} %copy.34, bf16[128,4096]{1,0:T(8,128)(2,1)S(1)} %copy-done.31, f32[128]{0:T(128)S(1)} %add_rsqrt_fusion.7, f32[4096]{0:T(1024)S(1)} %bitcast.606), kind=kOutput, calls=%fused_computation.2 | convolution fusion | flops 1612709888 | bytes 14434816 | tf_op jit(solution)/shard_map/dot_general | solution.py:83
  331.1 7.6 all_gather.87
  348.9 8.1 all_gather.88
  379.5 6.4 psum.22
  392.8 45.2 %all-gather.17.cloned.1.call-done = bf16[4,3,512,512]{3,2,1,0:T(8,128)(2,1)} async-done(((bf16[1,3,512,512]{3,2,1,0:T(8,128)(2,1)}), bf16[4,3,512,512]{3,2,1,0:T(8,128)(2,1)}) %all-gather.17.cloned.1.call-update) | async-done | bytes 6291472 | tf_op jit(solution)/shard_map/all_gather | solution.py:53
  456.1 45.0 %all-gather.19.cloned.1.call-done = bf16[4,3,512,512]{3,2,1,0:T(8,128)(2,1)} async-done(((bf16[1,3,512,512]{3,2,1,0:T(8,128)(2,1)}), bf16[4,3,512,512]{3,2,1,0:T(8,128)(2,1)}) %all-gather.19.cloned.1.call-update) | async-done | bytes 6291472 | tf_op jit(solution)/shard_map/all_gather | solution.py:53
  514.3 8.9 %all_gather.93 = bf16[512,768]{0,1:T(8,128)(2,1)S(1)} all-gather(bf16[512,192]{0,1:T(8,128)(2,1)} %fusion.147), channel_id=1, replica_groups=mesh['segment'=2,'seq'=4,'head'=4] {'seq'}, dimensions={1}, use_global_device_ids=true | all-gather | bytes 983040 | tf_op jit(solution)/shard_map/all_gather | solution.py:72
  524.5 8.7 all_gather.91
  534.1 8.8 all_gather.92
  551.5 27.4 %reduce-scatter.6.cloned.1.call-done = bf16[128,1024]{1,0:T(8,128)(2,1)} async-done(((bf16[128,4096]{1,0:T(8,128)(2,1)}), bf16[128,1024]{1,0:T(8,128)(2,1)}) %reduce-scatter.6.cloned.1.call-update) | async-done | bytes 262160 | tf_op jit(solution)/shard_map/reduce_scatter | solution.py:127
  590.8 28.0 %all-gather.21.cloned.1.call-done = bf16[128,4096]{1,0:T(8,128)(2,1)} async-done(((bf16[128,1024]{1,0:T(8,128)(2,1)}), bf16[128,4096]{1,0:T(8,128)(2,1)}) %all-gather.21.cloned.1.call-update) | async-done | bytes 1048592 | tf_op jit(solution)/shard_map/all_gather | solution.py:81
  620.5 9.0 %fusion = f32[128,3,512]{2,0,1:T(8,128)S(1)} fusion(bf16[1,4096,1,3,512]{1,4,3,2,0:T(8,128)(2,1)} %copy.34, bf16[128,4096]{1,0:T(8,128)(2,1)S(1)} %copy-done.30, f32[128]{0:T(128)S(1)} %add_rsqrt_fusion.3, f32[4096]{0:T(1024)S(1)} %bitcast.607), kind=kOutput, calls=%fused_computation | convolution fusion | flops 1612709888 | bytes 14434816 | tf_op jit(solution)/shard_map/dot_general | solution.py:83
  629.7 7.7 all_gather.95
  649.1 8.1 all_gather.96
  691.4 45.0 %all-gather.23.cloned.1.call-done = bf16[4,3,512,512]{3,2,1,0:T(8,128)(2,1)} async-done(((bf16[1,3,512,512]{3,2,1,0:T(8,128)(2,1)}), bf16[4,3,512,512]{3,2,1,0:T(8,128)(2,1)}) %all-gather.23.cloned.1.call-update) | async-done | bytes 6291472 | tf_op jit(solution)/shard_map/all_gather | solution.py:53
  753.5 46.5 %all-gather.25.cloned.1.call-done = bf16[4,3,512,512]{3,2,1,0:T(8,128)(2,1)} async-done(((bf16[1,3,512,512]{3,2,1,0:T(8,128)(2,1)}), bf16[4,3,512,512]{3,2,1,0:T(8,128)(2,1)}) %all-gather.25.cloned.1.call-update) | async-done | bytes 6291472 | tf_op jit(solution)/shard_map/all_gather | solution.py:53
  813.6 8.8 all_gather.101
  824.4 8.7 all_gather.99
  834.3 8.9 %all_gather.100 = bf16[512,768]{0,1:T(8,128)(2,1)S(1)} all-gather(bf16[512,192]{0,1:T(8,128)(2,1)S(1)} %fusion.142), channel_id=1, replica_groups=mesh['segment'=2,'seq'=4,'head'=4] {'seq'}, dimensions={1}, use_global_device_ids=true | all-gather | bytes 983040 | tf_op jit(solution)/shard_map/all_gather | solution.py:71
  853.1 27.4 %reduce-scatter.8.cloned.1.call-done = bf16[128,1024]{1,0:T(8,128)(2,1)} async-done(((bf16[128,4096]{1,0:T(8,128)(2,1)}), bf16[128,1024]{1,0:T(8,128)(2,1)}) %reduce-scatter.8.cloned.1.call-update) | async-done | bytes 262160 | tf_op jit(solution)/shard_map/reduce_scatter | solution.py:127
  (377 shorter events, 269.4 us)
Async XLA Ops:
  6.5 33.1 %all-gather.27.cloned.1.call-start = ((), (), s32[]{:S(2)}) async-start(), calls=%async_computation.23 | async-start | bytes 1310720 | tf_op jit(solution)/shard_map/all_gather | solution.py:81
  8.3 33.0 %copy-start.51 = (f32[1,4096]{1,0:T(1,128)S(1)}, f32[1,4096]{1,0:T(1,128)}, u32[]{:S(2)}) copy-start(f32[1,4096]{1,0:T(1,128)} %param.11) | copy-start | bytes 49156
  55.0 21.2 %all-to-all-start = ((bf16[128,4,192]{0,2,1:T(8,128)(2,1)}), bf16[128,4,192]{0,2,1:T(8,128)(2,1)S(1)}, u32[]{:S(2)}, u32[]{:S(2)}) async-start(bf16[128,4,192]{0,2,1:T(8,128)(2,1)} %bitcast.19), calls=%async_computation | async-start | bytes 393216 | tf_op jit(solution)/shard_map/all_to_all | solution.py:110
  76.2 8.6 all-to-all-start.1
  84.9 8.6 all-to-all-start.2
  88.2 63.8 %all-gather.11.cloned.1.call-start = ((), (), s32[]{:S(2)}) async-start(), calls=%async_computation.12 | async-start | bytes 7864320 | tf_op jit(solution)/shard_map/all_gather | solution.py:53
  106.8 101.6 %all-gather.13.cloned.1.call-start = ((), (), s32[]{:S(2)}) async-start(), calls=%async_computation.13 | async-start | bytes 7864320 | tf_op jit(solution)/shard_map/all_gather | solution.py:53
  161.9 117.8 %reduce-scatter.4.cloned.1.call-start = ((), (), s32[]{:S(2)}) async-start(), calls=%async_computation.14 | async-start | bytes 1310720 | tf_op jit(solution)/shard_map/reduce_scatter | solution.py:127
  243.9 95.4 %copy-start.70 = (f32[512]{0:T(512)}, f32[512]{0:T(512)S(1)}, u32[]{:S(2)}) copy-start(f32[512]{0:T(512)S(1)} %add_divide_fusion.11) | copy-start | bytes 6148
  244.4 95.4 %copy-start.52 = (f32[768]{0:T(1024)}, f32[768]{0:T(1024)S(1)}, u32[]{:S(2)}) copy-start(f32[768]{0:T(1024)S(1)} %add_divide_fusion.8) | copy-start | bytes 9220
  244.9 93.8 %copy-start.64 = (f32[768]{0:T(1024)}, f32[768]{0:T(1024)S(1)}, u32[]{:S(2)}) copy-start(f32[768]{0:T(1024)S(1)} %add_divide_fusion.7) | copy-start | bytes 9220
  252.2 67.5 %all-gather.15.cloned.1.call-start = ((), (), s32[]{:S(2)}) async-start(), calls=%async_computation.15 | async-start | bytes 1310720 | tf_op jit(solution)/shard_map/all_gather | solution.py:81
  281.5 8.5 collective-permute-start
  342.1 14.9 %all-to-all-start.3 = ((bf16[128,4,192]{0,2,1:T(8,128)(2,1)}), bf16[128,4,192]{0,2,1:T(8,128)(2,1)S(1)}, u32[]{:S(2)}, u32[]{:S(2)}) async-start(bf16[128,4,192]{0,2,1:T(8,128)(2,1)} %bitcast.54), calls=%async_computation.4 | async-start | bytes 393216 | tf_op jit(solution)/shard_map/all_to_all | solution.py:110
  357.0 8.6 all-to-all-start.4
  365.7 8.6 all-to-all-start.5
  369.1 68.9 %all-gather.17.cloned.1.call-start = ((), (), s32[]{:S(2)}) async-start(), calls=%async_computation.16 | async-start | bytes 7864320 | tf_op jit(solution)/shard_map/all_gather | solution.py:53
  392.7 108.4 %all-gather.19.cloned.1.call-start = ((), (), s32[]{:S(2)}) async-start(), calls=%async_computation.17 | async-start | bytes 7864320 | tf_op jit(solution)/shard_map/all_gather | solution.py:53
  454.6 124.3 %reduce-scatter.6.cloned.1.call-start = ((), (), s32[]{:S(2)}) async-start(), calls=%async_computation.18 | async-start | bytes 1310720 | tf_op jit(solution)/shard_map/reduce_scatter | solution.py:127
  524.5 113.9 %copy-start.80 = (f32[512]{0:T(512)}, f32[512]{0:T(512)S(1)}, u32[]{:S(2)}) copy-start(f32[512]{0:T(512)S(1)} %add_divide_fusion.10) | copy-start | bytes 6148
  534.1 105.2 %copy-start.78 = (f32[768]{0:T(1024)}, f32[768]{0:T(1024)S(1)}, u32[]{:S(2)}) copy-start(f32[768]{0:T(1024)S(1)} %add_divide_fusion.6) | copy-start | bytes 9220
  543.9 93.6 %copy-start.76 = (f32[768]{0:T(1024)}, f32[768]{0:T(1024)S(1)}, u32[]{:S(2)}) copy-start(f32[768]{0:T(1024)S(1)} %add_divide_fusion.5) | copy-start | bytes 9220
  549.7 29.2 %copy-start.35 = (bf16[128,1024]{1,0:T(8,128)(2,1)S(1)}, bf16[128,1024]{1,0:T(8,128)(2,1)}, u32[]{:S(2)}) copy-start(bf16[128,1024]{1,0:T(8,128)(2,1)} %bitcast_select_fusion.1) | copy-start | bytes 786436
  551.4 67.4 %all-gather.21.cloned.1.call-start = ((), (), s32[]{:S(2)}) async-start(), calls=%async_computation.19 | async-start | bytes 1310720 | tf_op jit(solution)/shard_map/all_gather | solution.py:81
  580.6 8.5 collective-permute-start.1
  642.3 14.9 %all-to-all-start.6 = ((bf16[128,4,192]{0,2,1:T(8,128)(2,1)}), bf16[128,4,192]{0,2,1:T(8,128)(2,1)S(1)}, u32[]{:S(2)}, u32[]{:S(2)}) async-start(bf16[128,4,192]{0,2,1:T(8,128)(2,1)} %bitcast.84), calls=%async_computation.8 | async-start | bytes 393216 | tf_op jit(solution)/shard_map/all_to_all | solution.py:110
  657.2 8.6 all-to-all-start.7
  665.8 8.6 all-to-all-start.8
  669.2 67.2 %all-gather.23.cloned.1.call-start = ((), (), s32[]{:S(2)}) async-start(), calls=%async_computation.20 | async-start | bytes 7864320 | tf_op jit(solution)/shard_map/all_gather | solution.py:53
  691.2 108.7 %all-gather.25.cloned.1.call-start = ((), (), s32[]{:S(2)}) async-start(), calls=%async_computation.21 | async-start | bytes 7864320 | tf_op jit(solution)/shard_map/all_gather | solution.py:53
  753.5 127.1 %reduce-scatter.8.cloned.1.call-start = ((), (), s32[]{:S(2)}) async-start(), calls=%async_computation.22 | async-start | bytes 1310720 | tf_op jit(solution)/shard_map/reduce_scatter | solution.py:127
  851.3 29.3 %copy-start.34 = (bf16[128,1024]{1,0:T(8,128)(2,1)S(1)}, bf16[128,1024]{1,0:T(8,128)(2,1)}, u32[]{:S(2)}) copy-start(bf16[128,1024]{1,0:T(8,128)(2,1)} %bitcast_select_fusion) | copy-start | bytes 786436
  (83 other events, 627.8 us)
Sparse Core Ops, SparseCore 0:
  8.9 30.6 all-gather.26
  107.0 45.0 all-gather.10
  162.0 46.3 all-gather.12
  252.4 27.2 reduce-scatter.3
  291.8 27.8 all-gather.14
  392.8 45.0 all-gather.16
  454.7 46.3 all-gather.18
  551.6 27.2 reduce-scatter.5
  591.0 27.8 all-gather.20
  691.3 45.0 all-gather.22
  753.6 46.3 all-gather.24
  853.2 27.3 reduce-scatter.7
